TPU v7x, 1024 devices: a whole 4x8x16 slice. The times are simulated.
1024 devices in a mesh: dp: 16 (over z), rep: 16 (over x, y_lo, core), mp: 4 (over y_hi).
Axes of the slice: x: 4, y: 8 (y_hi: 4, y_lo: 2; y = y_hi * 2 + y_lo), z: 16, core: 2. Of those that a mesh axis runs over, the one named last changes fastest.
Arguments:
- kv_weight: bfloat16 [512, 128, 256], P(('dp', 'mp')), may hold values from -0.25 to 0.25
- queries: bfloat16 [16, 128, 192], P('rep', 'dp'), may hold values from -8 to 8, as said below
- kv_cache: bfloat16 [16, 4096, 576], P('rep', 'mp'), may hold values from -8 to 8, as said below
- lengths: int32 [16], P('rep'), may hold values from 1024 to 4096, as said below
Outputs:
- rollout_weight: bfloat16 [512, 128, 256], P(None, 'dp')
- attn_out: bfloat16 [16, 128, 128], P('rep', 'dp')
Inputs may be any that keep to these rules, and one draw needn't show every extreme that they name: `lengths`: each request attends to cache positions 0 to its length - 1; some request has the full 4096. `queries`: entries are of order one. `kv_cache`: entries are of order one.
All inputs are finite; a program needn't handle non-finite values.
Results may differ from a plain program's by a relative error of at most 0.0072.
Values may be sent and summed in bfloat16 or wider, within the bound.
A program may use at most 32 MiB of HBM per device.

v0:
```python
import jax
import jax.numpy as jnp
from jax import lax
from jax.sharding import PartitionSpec as P

KVL = 512
NOPE = 128
ROPE = 64


def combined_all(part, axis, combine):
    gathered = jax.tree.map(lambda a: lax.all_gather(a, axis), part)

    def take(source):
        return jax.tree.map(lambda a: lax.dynamic_index_in_dim(a, source, 0, False), gathered)

    return lax.fori_loop(
        1, lax.axis_size(axis), lambda source, state: combine(state, take(source)), take(0)
    )


def combine_parts(earlier, later):
    top_one, total_one, value_one = earlier
    top_two, total_two, value_two = later
    top_score = jnp.maximum(top_one, top_two)
    factor_one = jnp.exp(top_one - top_score)
    factor_two = jnp.exp(top_two - top_score)
    total_sum = total_one * factor_one + total_two * factor_two
    merged = value_one * factor_one[:, :, None] + value_two * factor_two[:, :, None]
    return (top_score, total_sum, merged)


def per_device(kv_weight, queries, kv_cache, lengths):
    row_group = lax.all_gather(kv_weight, "mp", axis=0, tiled=True)
    local_weight = lax.all_to_all(row_group, "dp", split_axis=1, concat_axis=0, tiled=True)
    key_weight = local_weight[:, :, :NOPE]
    value_weight = local_weight[:, :, NOPE:]
    absorbed = jnp.einsum(
        "rhd,lhd->rhl", queries[:, :, :NOPE], key_weight, preferred_element_type=jnp.float32
    ).astype(jnp.bfloat16)
    full_query = jnp.concatenate([absorbed, queries[:, :, NOPE:]], axis=-1)
    scale = (NOPE + ROPE) ** (-0.5)
    scores = (
        jnp.einsum("rhc,rpc->rhp", full_query, kv_cache, preferred_element_type=jnp.float32) * scale
    )
    position_count = kv_cache.shape[1]
    positions = lax.axis_index("mp") * position_count + jnp.arange(position_count, dtype=jnp.int32)
    validity = positions[None, None, :] < lengths[:, None, None]
    masked = jnp.where(validity, scores, -1e30)
    top_score = jnp.max(masked, axis=-1)
    expd = jnp.where(validity, jnp.exp(masked - top_score[:, :, None]), 0.0)
    total_sum = jnp.sum(expd, axis=-1)
    soft_weights = expd.astype(jnp.bfloat16)
    latent_sum = jnp.einsum(
        "rhp,rpl->rhl", soft_weights, kv_cache[:, :, :KVL], preferred_element_type=jnp.float32
    )
    partial_value = jnp.einsum(
        "rhl,lhv->rhv",
        latent_sum,
        value_weight.astype(jnp.float32),
        precision=lax.Precision.HIGHEST,
    )
    merged_top, merged_total, merged_value = combined_all(
        (top_score, total_sum, partial_value), "mp", combine_parts
    )
    attn_out = (merged_value / merged_total[:, :, None]).astype(jnp.bfloat16)
    return (local_weight, attn_out)


def solution(mesh):
    in_specs = (P(("dp", "mp"), None, None), P("rep", "dp", None), P("rep", "mp", None), P("rep"))
    out_specs = (P(None, "dp", None), P("rep", "dp", None))
    return jax.shard_map(
        per_device, mesh=mesh, in_specs=in_specs, out_specs=out_specs, check_vma=False
    )
```

profile of v0, /device:TPU:2, one launch (start us, length us, event | category | flops | bytes accessed | tf_op | source)
XLA Modules:
  0.0 229.4 jit_solution(8904545829945041437)
XLA Ops:
  7.2 0.7 all-gather.5.cloned.1.call-update
  7.9 65.6 %all-gather.5.cloned.1.call-done = bf16[32,128,256]{2,1,0:T(8,128)(2,1)} async-done(((bf16[8,128,256]{2,1,0:T(8,128)(2,1)}), bf16[32,128,256]{2,1,0:T(8,128)(2,1)}) %all-gather.5.cloned.1.call-update) | async-done | bytes 2097168 | tf_op jit(solution)/shard_map/all_gather | solution.py:34
  73.5 4.1 %copy.9 = bf16[32,128,256]{2,0,1:T(8,128)(2,1)} copy(bf16[32,128,256]{2,1,0:T(8,128)(2,1)} %all-gather.5.cloned.1.call-done) | data formatting | bytes 4194304 | tf_op jit(solution)/shard_map/all_gather | solution.py:34
  77.6 13.0 %all-to-all-start = ((bf16[32,128,256]{2,0,1:T(8,128)(2,1)}), bf16[32,128,256]{2,0,1:T(8,128)(2,1)S(1)}, u32[]{:S(2)}, u32[]{:S(2)}) async-start(bf16[32,128,256]{2,0,1:T(8,128)(2,1)} %copy.9), calls=%async_computation | async-start | bytes 4194304 | tf_op jit(solution)/shard_map/all_to_all | solution.py:35
  91.2 1.3 dynamic-slice
  93.2 92.8 %all-to-all-done = bf16[32,128,256]{2,0,1:T(8,128)(2,1)S(1)} async-done(((bf16[32,128,256]{2,0,1:T(8,128)(2,1)}), bf16[32,128,256]{2,0,1:T(8,128)(2,1)S(1)}, u32[]{:S(2)}, u32[]{:S(2)}) %all-to-all-start) | async-done | bytes 2097184 | tf_op jit(solution)/shard_map/all_to_all | solution.py:35
  186.0 1.4 copy.10
  187.5 0.1 fusion.36
  187.6 1.2 copy-done
  188.8 0.4 fusion.19
  189.2 0.9 copy-done.1
  190.0 0.4 fusion.37
  190.4 0.2 fusion.23
  190.6 0.2 dynamic-update-slice
  190.9 0.2 dynamic-update-slice.1
  191.1 15.5 %all-reduce.2 = (f32[32]{0:T(128)S(1)}, f32[32]{0:T(128)S(1)}) all-reduce(f32[32]{0:T(128)S(1)} %dynamic-update-slice, f32[32]{0:T(128)S(1)} %dynamic-update-slice.1), channel_id=2, replica_groups=mesh['dp'=16,'rep'=16,'mp'=4] {'mp'}, use_global_device_ids=true, to_apply=%add | all-reduce | flops 64 | bytes 512
  206.6 0.1 reshape.116
  206.7 0.1 reshape.117
  206.7 0.4 convolution_bitcast_fusion
  207.1 0.6 fusion.17
  207.7 13.8 %all-gather.2 = f32[32,128]{1,0:T(8,128)S(1)} all-gather(f32[8,128]{1,0:T(8,128)S(1)} %bitcast.90), channel_id=4, replica_groups=mesh['dp'=16,'rep'=16,'mp'=4] {'mp'}, dimensions={0}, use_global_device_ids=true | all-gather | bytes 20480 | tf_op jit(solution)/shard_map/all_gather | solution.py:12
  221.5 0.3 while.19
  221.7 0.1 fusion.43
  221.9 0.7 divide_convert_fusion
  (25 shorter events, 0.3 us)
Async XLA Ops:
  7.2 66.3 %all-gather.5.cloned.1.call-start = ((), (), s32[]{:S(2)}) async-start(), calls=%async_computation.1 | async-start | bytes 2621440 | tf_op jit(solution)/shard_map/all_gather | solution.py:34
  77.6 15.6 %copy-start.2 = (bf16[1,8,192]{2,1,0:T(8,128)(2,1)S(1)}, bf16[1,8,192]{2,1,0:T(8,128)(2,1)}, u32[]{:S(2)}) copy-start(bf16[1,8,192]{2,1,0:T(8,128)(2,1)} %param.7) | copy-start | bytes 9220
  77.6 108.5 %all-to-all-start = ((bf16[32,128,256]{2,0,1:T(8,128)(2,1)}), bf16[32,128,256]{2,0,1:T(8,128)(2,1)S(1)}, u32[]{:S(2)}, u32[]{:S(2)}) async-start(bf16[32,128,256]{2,0,1:T(8,128)(2,1)} %copy.9), calls=%async_computation | async-start | bytes 4194304 | tf_op jit(solution)/shard_map/all_to_all | solution.py:35
  187.5 1.3 copy-start
  188.8 1.3 copy-start.1
  188.8 1.3 slice-start
Sparse Core Ops, SparseCore 0:
  10.7 62.7 all-gather.4
where the time goes:
time: 230 us; the launch traced here: 229 us
  waiting for transfers between devices  159 us (69%)
  blocking collectives  29.3 us (13%)
  between operations  15.4 us (7%)
  starting transfers between devices  13 us (6%)
  local copies, waits for them, and re-layouts  9.64 us (4%)
    all_to_all x1, waiting for transfers between devices, per_device(): lax.all_to_all(row_group, 'dp', split_axis=1, concat_axis=0, tiled=True)  92.8 us
    all_gather x1, waiting for transfers between devices, per_device(): row_group = lax.all_gather(kv_weight, 'mp', axis=0, tiled=True)  65.6 us
    unnamed x1, blocking collectives  15.5 us
    all_gather x1, blocking collectives, combined_all(): gathered = jax.tree.map(lambda a: lax.all_gather(a, axis), part)  13.8 us
    all_to_all x1, starting transfers between devices, per_device(): lax.all_to_all(row_group, 'dp', split_axis=1, concat_axis=0, tiled=True)  13 us
  transfers between devices with their start and end apart: 2, of which 2 were waited for; matrix products, arithmetic and copies ran while one was open for 1% of the time, Pallas kernels for 0%

commit v1 on v0

v1 whole, which is shorter than its diff:
```python
import functools

import jax
import jax.numpy as jnp
from jax import lax
from jax.experimental import pallas as pl
from jax.experimental.pallas import tpu as pltpu
from jax.sharding import PartitionSpec as P

KVL = 512
NOPE = 128
ROPE = 64
VDIM = 128
WIDTH = NOPE + VDIM
NZ = 16
NY = 8
HPD = 8
MESH = pl.DeviceIdType.MESH

GROUPS = ((6, 11, 2.5), (4, 6, 4.2), (11, 13, 4.3), (13, 16, 7.4), (0, 4, 8.2))
HOP = 2.0


def spread(rows, cols, test):
    r = lax.broadcasted_iota(jnp.int32, (rows, cols), 0)
    c = lax.broadcasted_iota(jnp.int32, (rows, cols), 1)
    return jnp.where(test(r, c), 1.0, 0.0).astype(jnp.bfloat16)


def gather_kernel(
    kvw, qh, kth, lens, w, lat,
    share, relay, kt, qv, qall, ab_send, ab_recv, mg_send, mg_recv,
    loc_sem, z_send, z_recv, r_send, r_recv, f_send, q_send, q_recv,
    y_send, y_recv, c_send, c_recv, a_send, a_recv, m_send, m_recv,
):
    z = lax.axis_index("dp")
    k = lax.axis_index("rep")
    m = lax.axis_index("mp")
    x = k // 4
    ylo = (k // 2) % 2
    c = k % 2
    y = 2 * m + ylo
    s = 2 * ylo + c
    me = 2 * y + c
    sg = 1 - 2 * c

    def dev(zz, yy, cc):
        return {"dp": zz, "rep": x * 4 + (yy % 2) * 2 + cc, "mp": yy // 2}

    def zdev(d):
        return dev((z + d + NZ) % NZ, y, c)

    def remote(src, dst, send, recv, to):
        return pltpu.make_async_remote_copy(
            src_ref=src, dst_ref=dst, send_sem=send, recv_sem=recv, device_id=to, device_id_type=MESH
        )

    fetch_share = pltpu.make_async_copy(kvw.at[pl.ds(2 * s, 2)], share, loc_sem.at[0])
    fetch_kt = pltpu.make_async_copy(kth.at[0], kt, loc_sem.at[1])
    fetch_q = pltpu.make_async_copy(qh.at[0], qv, loc_sem.at[2])
    fetch_share.start()
    fetch_q.start()

    barrier = pltpu.get_barrier_semaphore()
    for d in (4, -4, 3, -3, 2, -2, 1, -1):
        pl.semaphore_signal(barrier, inc=1, device_id=zdev(d), device_id_type=MESH)
    for dy in range(NY):
        for dc in range(2):
            if dy or dc:
                to = dev(z, (y + dy) % NY, (c + dc) % 2)
                pl.semaphore_signal(barrier, inc=1, device_id=to, device_id_type=MESH)
    fetch_kt.start()
    fetch_share.wait()
    fetch_q.wait()
    own_q = pltpu.make_async_copy(qh.at[0, :, pl.ds(0, NOPE)], qall.at[s], loc_sem.at[3])
    own_q.start()
    own_w = pltpu.make_async_copy(share.at[:, z], w.at[8, y, c], loc_sem.at[4])
    own_w.start()
    pl.semaphore_wait(barrier, 8 + 15)

    started = []

    def piece(d):
        return share.at[:, (z + d + NZ) % NZ]

    far = [5, -5, 6, -6, 7, -7, 8]
    relays = {}
    for n, d in enumerate(far):
        step = 4 if d > 0 else -4
        cp = remote(piece(d), relay.at[n], r_send.at[n], r_recv.at[n], zdev(step))
        cp.start()
        relays[d] = cp
        started.append(cp)
    near = {}
    for n, d in enumerate((4, -4, 3, -3, 2, -2, 1, -1)):
        cp = remote(piece(d), w.at[8 - d, y, c], z_send.at[n], z_recv.at[8 - d], zdev(d))
        cp.start()
        near[d] = cp
        started.append(cp)

    q_in = []
    for n, (dl, dc) in enumerate(((0, 1), (1, 0), (1, 1))):
        to = dev(z, 2 * m + (ylo + dl) % 2, (c + dc) % 2)
        cp = remote(qv.at[:, pl.ds(0, NOPE)], qall.at[s], q_send.at[n], q_recv.at[n], to)
        cp.start()
        q_in.append(cp)
        started.append(cp)

    arrived = {}

    def z_wait(slot):
        if slot == 8:
            own_w.wait()
        elif 4 <= slot <= 12:
            near[8 - slot].wait_recv()
        else:
            forwards[8 - slot].wait_recv()

    forwards = {}

    def forward_far():
        for n, d in enumerate(far):
            relays[d].wait_recv()
            rest = d - 4 if d > 0 else d + 4
            cp = remote(relay.at[n], w.at[8 - d, y, c], f_send.at[n], z_recv.at[8 - d], zdev(rest))
            cp.start()
            forwards[d] = cp
            started.append(cp)

    core_in = []

    def to_core(g, src, n):
        lo, hi, _ = GROUPS[g]
        ref = w.at[pl.ds(lo, hi - lo), src, c]
        cp = remote(ref, ref, c_send.at[g, n], c_recv.at[g, n], dev(z, y, 1 - c))
        cp.start()
        core_in.append(cp)
        started.append(cp)

    def to_y(g, src, n, sign):
        lo, hi, _ = GROUPS[g]
        ref = w.at[pl.ds(lo, hi - lo), src, c]
        cp = remote(ref, ref, y_send.at[g, n], y_recv.at[g, n], dev(z, (y + sign * sg + NY) % NY, c))
        cp.start()
        arrived[g, n] = cp
        started.append(cp)

    def ready(g):
        lo, hi, _ = GROUPS[g]
        for slot in range(lo, hi):
            z_wait(slot)
        to_y(g, y, 0, 1)
        to_y(g, y, 4, -1)
        to_core(g, y, 0)

    def relay_y(g, step, sign):
        n = step - 1 if sign > 0 else 3 + step
        arrived[g, n].wait_recv()
        src = (y - sign * step * sg + 2 * NY) % NY
        if step < (4 if sign > 0 else 3):
            to_y(g, src, n + 1, sign)
        to_core(g, src, n + 1)

    def absorb():
        for cp in q_in:
            cp.wait_recv()
        own_q.wait()
        keys = w[:, y, c, :, :, 0:NOPE].astype(jnp.float32).reshape(2 * NZ * HPD, NOPE)
        ask = qall[...].astype(jnp.float32).reshape(4 * HPD, NOPE)
        cross = lax.dot_general(
            ask.astype(jnp.bfloat16), keys.astype(jnp.bfloat16), (((1,), (1,)), ((), ())),
            preferred_element_type=jnp.float32,
        )
        r = lax.broadcasted_iota(jnp.int32, cross.shape, 0)
        cc = lax.broadcasted_iota(jnp.int32, cross.shape, 1)
        own = jnp.where(r % HPD == cc % HPD, cross, 0.0).astype(jnp.bfloat16)
        base = 32 * (me % 4)
        pick = spread(2 * NZ * HPD, 128, lambda i, j: j == base + i // HPD)
        packed = jnp.dot(own, pick, preferred_element_type=jnp.float32)
        ab_send[...] = packed.reshape(4, HPD, 128).astype(jnp.bfloat16)
        for n in range(1, 16):
            dy, dc = n // 2, n % 2
            yy, cc2 = (y + dy) % NY, (c + dc) % 2
            cp = remote(
                ab_send.at[2 * (yy % 2) + cc2], ab_recv.at[me], a_send.at[n], a_recv.at[n], dev(z, yy, cc2)
            )
            cp.start()
            ab_in.append(cp)
            started.append(cp)
        own_ab = pltpu.make_async_copy(ab_send.at[s], ab_recv.at[me], loc_sem.at[5])
        own_ab.start()
        ab_own.append(own_ab)

    ab_in, ab_own, mg_in = [], [], []

    def attend():
        def place(i, j):
            src, slot, row = i // 32, (i % 32) // 2, i % 2
            return j == ((slot + z + 8) % NZ) * 32 + src * 2 + row

        perm = spread(KVL, KVL, place)
        fetch_kt.wait()
        ab_own[0].wait()
        for cp in ab_in:
            cp.wait_recv()
        tiles = [
            sum(ab_recv[4 * g + j].astype(jnp.float32) for j in range(4)) for g in range(4)
        ]
        got = jnp.concatenate(tiles, axis=1).astype(jnp.bfloat16)
        absorbed = jnp.dot(got, perm, preferred_element_type=jnp.float32).astype(jnp.bfloat16)
        scores = jnp.dot(absorbed, kt[0:KVL, :], preferred_element_type=jnp.float32)
        scores += jnp.dot(qv[:, NOPE : NOPE + ROPE], kt[KVL : KVL + ROPE, :], preferred_element_type=jnp.float32)
        scores = scores * ((NOPE + ROPE) ** (-0.5))
        count = kt.shape[1]
        positions = m * count + lax.broadcasted_iota(jnp.int32, scores.shape, 1)
        valid = positions < lens[0]
        masked = jnp.where(valid, scores, -1e30)
        top = jnp.max(masked, axis=1, keepdims=True)
        expd = jnp.where(valid, jnp.exp(masked - top), 0.0)
        total = jnp.sum(expd, axis=1, keepdims=True)
        part = lax.dot_general(
            expd.astype(jnp.bfloat16), kt[0:KVL, :], (((1,), (1,)), ((), ())),
            preferred_element_type=jnp.float32,
        )
        lane = lax.broadcasted_iota(jnp.int32, (HPD, 128), 1)
        mg_send[:, 0:KVL] = part
        mg_send[:, KVL : KVL + 128] = jnp.where(lane < 64, top, total)
        for n in range(1, 4):
            cp = remote(
                mg_send, mg_recv.at[n - 1], m_send.at[n], m_recv.at[n], dev(z, (y + 2 * n) % NY, c)
            )
            cp.start()
            mg_in.append(cp)
            started.append(cp)

    def merge():
        for cp in mg_in:
            cp.wait_recv()
        parts = [mg_send[...]] + [mg_recv[n] for n in range(3)]
        tops = [p[:, KVL : KVL + 1] for p in parts]
        totals = [p[:, KVL + 64 : KVL + 65] for p in parts]
        top = jnp.maximum(jnp.maximum(tops[0], tops[1]), jnp.maximum(tops[2], tops[3]))
        factors = [jnp.exp(t - top) for t in tops]
        total = sum(f * t for f, t in zip(factors, totals))
        value = sum(f * p[:, 0:KVL] for f, p in zip(factors, parts))
        lat[...] = value / total

    events = [(3.9, forward_far), (8.7, absorb), (13.5, attend), (19.0, merge)]
    for g, (_, _, at) in enumerate(GROUPS):
        events.append((at, functools.partial(ready, g)))
        for step in range(1, 5):
            events.append((at + step * HOP, functools.partial(relay_y, g, step, 1)))
            if step < 4:
                events.append((at + step * HOP, functools.partial(relay_y, g, step, -1)))
    events.sort(key=lambda e: e[0])
    for _, run in events:
        run()
    for cp in core_in:
        cp.wait_recv()
    for cp in started:
        cp.wait_send()


def project_kernel(w, lat, out, attn, sems):
    z = lax.axis_index("dp")
    copies = []
    for i in range(NZ):
        slot = (i - z + 8 + NZ) % NZ
        cp = pltpu.make_async_copy(w.at[slot], out.at[i], sems.at[i])
        cp.start()
        copies.append(cp)
    value = lat[...]
    high = value.astype(jnp.bfloat16)
    low = (value - high.astype(jnp.float32)).astype(jnp.bfloat16)
    both = jnp.concatenate([high.astype(jnp.float32), low.astype(jnp.float32)], axis=0).astype(jnp.bfloat16)
    widen = spread(128, 128 * HPD, lambda i, j: j // HPD == i)
    r = lax.broadcasted_iota(jnp.int32, (2 * HPD, 128 * HPD), 0)
    cc = lax.broadcasted_iota(jnp.int32, (2 * HPD, 128 * HPD), 1)
    diagonal = r % HPD == cc % HPD
    total = jnp.zeros((2 * HPD, VDIM), jnp.float32)
    for g in range(4):
        wide = jnp.dot(both[:, g * 128 : (g + 1) * 128], widen, preferred_element_type=jnp.float32)
        wide = jnp.where(diagonal, wide, 0.0).astype(jnp.bfloat16)
        for j in range(4):
            slot = (4 * g + j - z + 8 + NZ) % NZ
            vals = w[slot, :, :, :, :, NOPE:WIDTH].astype(jnp.float32).reshape(32 * HPD, VDIM)
            total += jnp.dot(
                wide[:, j * 256 : (j + 1) * 256], vals.astype(jnp.bfloat16), preferred_element_type=jnp.float32
            )
    attn[0] = (total[0:HPD] + total[HPD:]).astype(jnp.bfloat16)
    for cp in copies:
        cp.wait()


def per_device(kv_weight, queries, kv_cache, lengths):
    rows = kv_weight.shape[0]
    kvw = kv_weight.reshape(rows, NZ, HPD, WIDTH)
    kth = jnp.swapaxes(kv_cache, 1, 2)
    count = kth.shape[2]
    dma = pltpu.SemaphoreType.DMA
    groups = len(GROUPS)
    vmem = pl.BlockSpec(memory_space=pltpu.VMEM)
    hbm = pl.BlockSpec(memory_space=pl.ANY)
    w_shape = jax.ShapeDtypeStruct((NZ, NY, 2, 2, HPD, WIDTH), jnp.bfloat16)
    w, lat = pl.pallas_call(
        gather_kernel,
        out_shape=(w_shape, jax.ShapeDtypeStruct((HPD, KVL), jnp.float32)),
        in_specs=[hbm, hbm, hbm, pl.BlockSpec(memory_space=pltpu.SMEM)],
        out_specs=(vmem, vmem),
        scratch_shapes=[
            pltpu.VMEM((2, NZ, HPD, WIDTH), jnp.bfloat16),
            pltpu.VMEM((7, 2, HPD, WIDTH), jnp.bfloat16),
            pltpu.VMEM((KVL + ROPE, count), jnp.bfloat16),
            pltpu.VMEM((HPD, NOPE + ROPE), jnp.bfloat16),
            pltpu.VMEM((4, HPD, NOPE), jnp.bfloat16),
            pltpu.VMEM((4, HPD, 128), jnp.bfloat16),
            pltpu.VMEM((16, HPD, 128), jnp.bfloat16),
            pltpu.VMEM((HPD, KVL + 128), jnp.float32),
            pltpu.VMEM((3, HPD, KVL + 128), jnp.float32),
            dma((6,)), dma((8,)), dma((16,)), dma((7,)), dma((7,)), dma((7,)), dma((3,)), dma((3,)),
            dma((groups, 7)), dma((groups, 7)), dma((groups, 8)), dma((groups, 8)),
            dma((16,)), dma((16,)), dma((4,)), dma((4,)),
        ],
        compiler_params=pltpu.CompilerParams(collective_id=0, has_side_effects=True),
        name="gather",
    )(kvw, queries, kth, lengths)
    out, attn = pl.pallas_call(
        project_kernel,
        out_shape=(w_shape, jax.ShapeDtypeStruct((1, HPD, VDIM), jnp.bfloat16)),
        in_specs=[vmem, vmem],
        out_specs=(hbm, vmem),
        scratch_shapes=[dma((NZ,))],
        name="project",
    )(w, lat)
    return out.reshape(KVL, HPD, WIDTH), attn


def solution(mesh):
    in_specs = (P(("dp", "mp"), None, None), P("rep", "dp", None), P("rep", "mp", None), P("rep"))
    out_specs = (P(None, "dp", None), P("rep", "dp", None))
    return jax.shard_map(per_device, mesh=mesh, in_specs=in_specs, out_specs=out_specs, check_vma=False)
```

time: 230 us -> 62.3 us (0.27)
  the two profiles are of different devices: /device:TPU:2 before, /device:TPU:1 now
where the time goes in v1:
time: 62.3 us; the launch traced here: 62.1 us
  Pallas kernels  60.8 us (98%)
  between operations  1.28 us (2%)
    pallas_call x1, Pallas kernels, per_device(): pl.pallas_call(gather_kernel, out_shape=(w_shape, jax.ShapeDtypeStruct((H...  57.1 us
    pallas_call x1, Pallas kernels, per_device(): pl.pallas_call(project_kernel, out_shape=(w_shape, jax.ShapeDtypeStruct((...  3.66 us

profile of v1, /device:TPU:1, one launch (start us, length us, event | category | flops | bytes accessed | tf_op | source)
XLA Modules:
  0.0 62.1 jit_solution(14157362296631072450)
XLA Ops:
  1.3 57.1 %gather.1 = (bf16[16,8,2,2,8,256]{5,4,3,2,1,0:T(8,128)(2,1)}, f32[8,512]{1,0:T(8,128)}) custom-call(bf16[8,16,8,256]{3,2,1,0:T(8,128)(2,1)} %bitcast.4, bf16[1,8,192]{2,1,0:T(8,128)(2,1)} %qh.1, bf16[1,576,1024]{2,1,0:T(8,128)(2,1)} %bitcast.3, s32[1]{0:T(128)S(6)} %copy.6.lens), custom_call_target="tpu_custom_call" | custom-call | tf_op jit(solution)/shard_map/gather/pallas_call | solution.py:305
  58.4 3.7 %project.1 = (bf16[16,8,2,2,8,256]{5,4,3,2,1,0:T(8,128)(2,1)}, bf16[1,8,128]{2,1,0:T(8,128)(2,1)}) custom-call(bf16[16,8,2,2,8,256]{5,4,3,2,1,0:T(8,128)(2,1)} %get-tuple-element.6.w, f32[8,512]{1,0:T(8,128)} %get-tuple-element.7.lat), custom_call_target="tpu_custom_call" | custom-call | tf_op jit(solution)/shard_map/project/pallas_call | solution.py:327

commit v2 on v1

v2 whole, which is shorter than its diff:
```python
import functools

import jax
import jax.numpy as jnp
from jax import lax
from jax.experimental import pallas as pl
from jax.experimental.pallas import tpu as pltpu
from jax.sharding import PartitionSpec as P

KVL = 512
NOPE = 128
ROPE = 64
VDIM = 128
WIDTH = NOPE + VDIM
NX = 4
NY = 8
NZ = 16
HPD = 8
MESH = pl.DeviceIdType.MESH

NEAR, FAR = 0, 1
REACH = (4, -4, 3, -3, 2, -2, 1, -1)
FAR_D = (8, 7, -7, 6, -6, 5, -5)


def spread(rows, cols, test):
    r = lax.broadcasted_iota(jnp.int32, (rows, cols), 0)
    c = lax.broadcasted_iota(jnp.int32, (rows, cols), 1)
    return jnp.where(test(r, c), 1.0, 0.0).astype(jnp.bfloat16)


def gather_kernel(
    kvw, qh, kth, lenh, w, lat,
    share, zkeys, relay_k, relay_v, kt, qv, lens, qall, ab_send, ab_recv, mg_send, mg_recv,
    loc, zs, zn, zr, zf, fs, vs, vr, vq, qs, qr, ys, yr, xs, xf, xb, xq, cs, cr, a_s, a_r, m_s, m_r,
):
    z = lax.axis_index("dp")
    k = lax.axis_index("rep")
    m = lax.axis_index("mp")
    x = k // 4
    ylo = (k // 2) % 2
    c = k % 2
    y = 2 * m + ylo
    s = 2 * ylo + c
    me = 2 * y + c
    sg = 1 - 2 * c
    key = pl.ds(0, NOPE)
    pair = pl.ds(2 * c, 2)

    def dev(zz, yy, cc, xx=x):
        return {"dp": zz, "rep": xx * 4 + (yy % 2) * 2 + cc, "mp": yy // 2}

    def zdev(d):
        return dev((z + d + 2 * NZ) % NZ, y, c)

    def xdev(d):
        return dev(z, y, c, (x + d + NX) % NX)

    def remote(src, dst, send, recv, to):
        return pltpu.make_async_remote_copy(
            src_ref=src, dst_ref=dst, send_sem=send, recv_sem=recv, device_id=to, device_id_type=MESH
        )

    def local(src, dst, sem):
        return pltpu.make_async_copy(src, dst, sem)

    def wait_all(sem, ref):
        local(ref, ref, sem).wait()

    fetch_w = local(kvw.at[pl.ds(2 * s, 2)], share, loc.at[0])
    fetch_kt = local(kth.at[0], kt, loc.at[1])
    fetch_q = local(qh.at[0], qv, loc.at[2])
    fetch_l = local(lenh, lens, loc.at[3])
    fetch_w.start()
    fetch_q.start()

    barrier = pltpu.get_barrier_semaphore()
    for d in REACH:
        pl.semaphore_signal(barrier, inc=1, device_id=zdev(d), device_id_type=MESH)
    for n in range(1, 2 * NY):
        to = dev(z, (y + n // 2) % NY, (c + n % 2) % 2)
        pl.semaphore_signal(barrier, inc=1, device_id=to, device_id_type=MESH)
    for d in (1, -1):
        pl.semaphore_signal(barrier, inc=1, device_id=xdev(d), device_id_type=MESH)
    fetch_kt.start()
    fetch_l.start()
    fetch_w.wait()
    fetch_q.wait()
    own_q = local(qh.at[0, :, pl.ds(0, NOPE)], qall.at[s], loc.at[4])
    own_q.start()
    own_k = local(share.at[:, z, :, key], zkeys.at[4], loc.at[5])
    own_k.start()
    pl.semaphore_wait(barrier, len(REACH) + 15 + 2)

    def piece(d):
        return share.at[:, (z + d + 2 * NZ) % NZ]

    def key_piece(d):
        return share.at[:, (z + d + 2 * NZ) % NZ, :, key]

    for n, d in enumerate(FAR_D):
        remote(key_piece(d), relay_k.at[n], zs, zr, zdev(4 if d > 0 else -4)).start()
    for d in REACH:
        remote(key_piece(d), zkeys.at[(4 - d) % NZ], zs, zn, zdev(d)).start()
    up = remote(piece(8 - x), relay_v.at[1], vs.at[3], vq.at[1], zdev(4))
    down = remote(piece(-4 - x), relay_v.at[0], vs.at[2], vq.at[0], zdev(-4))
    ahead = remote(piece(4 - x), w.at[0, x, y, pair], vs.at[0], vr.at[0], zdev(4 - x))
    behind = remote(piece(-x), w.at[1, x, y, pair], vs.at[1], vr.at[1], zdev(-x))
    behind_own = local(piece(0), w.at[1, x, y, pair], vr.at[1])
    up.start()
    down.start()
    ahead.start()

    @pl.when(x > 0)
    def _():
        behind.start()

    @pl.when(x == 0)
    def _():
        behind_own.start()

    for dl, dc in ((0, 1), (1, 0), (1, 1)):
        to = dev(z, 2 * m + (ylo + dl) % 2, (c + dc) % 2)
        remote(qv.at[:, pl.ds(0, NOPE)], qall.at[s], qs, qr, to).start()

    up_rest = remote(relay_v.at[1], w.at[3, x, y, pair], vs.at[5], vr.at[3], zdev(4 - x))
    down_rest = remote(relay_v.at[0], w.at[2, x, y, pair], vs.at[4], vr.at[2], zdev(-x))
    down_own = local(relay_v.at[0], w.at[2, x, y, pair], vr.at[2])

    def forward_far():
        wait_all(zr, relay_k)
        for n, d in enumerate(FAR_D):
            rest = d - 4 if d > 0 else d + 4
            remote(relay_k.at[n], zkeys.at[(4 - d) % NZ], fs, zf, zdev(rest)).start()
        up.wait_recv()
        up_rest.start()
        down.wait_recv()

        @pl.when(x > 0)
        def _():
            down_rest.start()

        @pl.when(x == 0)
        def _():
            down_own.start()

    def chunk(g, src):
        return w.at[pl.ds(2 * g, 2), x, src, pair]

    def to_y(g):
        for n in (4, 3, 5, 2, 6, 1, 7):
            remote(chunk(g, y), chunk(g, y), ys.at[g], yr.at[g], dev(z, (y + n) % NY, c)).start()

    def near_ready():
        wait_all(zn, zkeys.at[pl.ds(0, 8)])
        own_k.wait()
        ahead.wait_recv()
        behind.wait_recv()
        to_y(NEAR)

    def far_keys():
        wait_all(zf, relay_k)

    def far_ready():
        up_rest.wait_recv()
        down_rest.wait_recv()
        to_y(FAR)

    def part(g, n, b):
        return w.at[2 * g + n // 2, b, pl.ds(4 * (n % 2), 4), pair]

    def to_x(g):
        wait_all(yr.at[g], w.at[0, 0, pl.ds(0, 7)])
        for n in range(4):
            ref = part(g, n, x)
            remote(ref, ref, xs.at[g], xf.at[g, n], xdev(sg)).start()
            remote(ref, ref, xs.at[g], xb.at[g], xdev(-sg)).start()
        to_core(g, x)

    def relay_x(g, n):
        ref = part(g, n, (x - sg + NX) % NX)
        cp = remote(ref, ref, xs.at[g], xf.at[g, n], xdev(sg))
        cp.wait_recv()
        remote(ref, ref, xs.at[g], xq.at[g], xdev(sg)).start()

    def to_core(g, b):
        ref = w.at[pl.ds(2 * g, 2), b, :, pair]
        remote(ref, ref, cs, cr, dev(z, y, 1 - c)).start()

    def behind_x(g):
        to_core(g, (x - sg + NX) % NX)

    def other_x(g):
        wait_all(xb.at[g], w.at[0, 0])
        to_core(g, (x + sg + NX) % NX)

    def across_x(g):
        wait_all(xq.at[g], w.at[0, 0])
        to_core(g, (x + 2) % NX)

    def absorb():
        wait_all(qr, qall.at[pl.ds(0, 3)])
        own_q.wait()
        keys = zkeys[...].astype(jnp.float32).reshape(2 * NZ * HPD, NOPE)
        ask = qall[...].astype(jnp.float32).reshape(4 * HPD, NOPE)
        cross = lax.dot_general(
            ask.astype(jnp.bfloat16), keys.astype(jnp.bfloat16), (((1,), (1,)), ((), ())),
            preferred_element_type=jnp.float32,
        )
        r = lax.broadcasted_iota(jnp.int32, cross.shape, 0)
        cc = lax.broadcasted_iota(jnp.int32, cross.shape, 1)
        own = jnp.where(r % HPD == cc % HPD, cross, 0.0).astype(jnp.bfloat16)
        base = 32 * (me % 4)
        pick = spread(2 * NZ * HPD, 128, lambda i, j: j == base + i // HPD)
        packed = jnp.dot(own, pick, preferred_element_type=jnp.float32)
        ab_send[...] = packed.reshape(4, HPD, 128).astype(jnp.bfloat16)
        own_ab.start()
        for n in (8, 9, 7, 10, 6, 11, 5, 12, 4, 13, 3, 14, 2, 15, 1):
            yy, cc2 = (y + n // 2) % NY, (c + n % 2) % 2
            remote(ab_send.at[2 * (yy % 2) + cc2], ab_recv.at[me], a_s, a_r, dev(z, yy, cc2)).start()

    own_ab = local(ab_send.at[s], ab_recv.at[me], loc.at[6])

    def attend():
        def place(i, j):
            src, slot, row = i // 32, (i % 32) // 2, i % 2
            return j == ((slot + z + 12) % NZ) * 32 + src * 2 + row

        perm = spread(KVL, KVL, place)
        fetch_kt.wait()
        fetch_l.wait()
        own_ab.wait()
        wait_all(a_r, ab_recv.at[pl.ds(0, 15)])
        tiles = [sum(ab_recv[4 * g + j].astype(jnp.float32) for j in range(4)) for g in range(4)]
        got = jnp.concatenate(tiles, axis=1).astype(jnp.bfloat16)
        absorbed = jnp.dot(got, perm, preferred_element_type=jnp.float32).astype(jnp.bfloat16)
        scores = jnp.dot(absorbed, kt[0:KVL, :], preferred_element_type=jnp.float32)
        scores += jnp.dot(qv[:, NOPE : NOPE + ROPE], kt[KVL : KVL + ROPE, :], preferred_element_type=jnp.float32)
        scores = scores * ((NOPE + ROPE) ** (-0.5))
        count = kt.shape[1]
        positions = m * count + lax.broadcasted_iota(jnp.int32, scores.shape, 1)
        valid = positions < lens[0]
        masked = jnp.where(valid, scores, -1e30)
        top = jnp.max(masked, axis=1, keepdims=True)
        expd = jnp.where(valid, jnp.exp(masked - top), 0.0)
        total = jnp.sum(expd, axis=1, keepdims=True)
        part = lax.dot_general(
            expd.astype(jnp.bfloat16), kt[0:KVL, :], (((1,), (1,)), ((), ())),
            preferred_element_type=jnp.float32,
        )
        lane = lax.broadcasted_iota(jnp.int32, (HPD, 128), 1)
        mg_send[:, 0:KVL] = part
        mg_send[:, KVL : KVL + 128] = jnp.where(lane < 64, top, total)
        for n in (2, 1, 3):
            to = dev(z, (y + 2 * n) % NY, c)
            remote(mg_send, mg_recv.at[n - 1], m_s, m_r, to).start()

    def merge():
        wait_all(m_r, mg_recv)
        parts = [mg_send[...]] + [mg_recv[n] for n in range(3)]
        tops = [p[:, KVL : KVL + 1] for p in parts]
        totals = [p[:, KVL + 64 : KVL + 65] for p in parts]
        top = jnp.maximum(jnp.maximum(tops[0], tops[1]), jnp.maximum(tops[2], tops[3]))
        factors = [jnp.exp(t - top) for t in tops]
        total = sum(f * t for f, t in zip(factors, totals))
        value = sum(f * p[:, 0:KVL] for f, p in zip(factors, parts))
        lat[...] = value / total

    forward_far()
    near_ready()
    far_keys()
    far_ready()
    absorb()
    to_x(NEAR)
    for n in range(4):
        relay_x(NEAR, n)
    attend()
    to_x(FAR)
    behind_x(NEAR)
    other_x(NEAR)
    across_x(NEAR)
    for n in range(4):
        relay_x(FAR, n)
    behind_x(FAR)
    other_x(FAR)
    merge()
    across_x(FAR)
    wait_all(cr, w.at[pl.ds(0, 2)])

    wait_all(zs, zkeys.at[pl.ds(0, 15)])
    wait_all(fs, relay_k)
    for cp in (up, down, ahead, up_rest):
        cp.wait_send()

    @pl.when(x > 0)
    def _():
        behind.wait_send()
        down_rest.wait_send()

    wait_all(qs, qall.at[pl.ds(0, 3)])
    for g in (NEAR, FAR):
        wait_all(ys.at[g], w.at[0, 0, pl.ds(0, 7)])
        wait_all(xs.at[g], w.at[0, pl.ds(0, 3)])
    wait_all(cs, w.at[pl.ds(0, 2)])
    wait_all(a_s, ab_recv.at[pl.ds(0, 15)])
    wait_all(m_s, mg_recv)


def project_kernel(w, lat, out, attn, sems):
    z = lax.axis_index("dp")
    copies = []
    for i in range(NZ):
        slot = (i - z + 4 + NZ) % NZ
        cp = pltpu.make_async_copy(w.at[slot // 4, slot % 4], out.at[i], sems.at[i])
        cp.start()
        copies.append(cp)
    value = lat[...]
    high = value.astype(jnp.bfloat16).astype(jnp.float32)
    both = jnp.concatenate([high, value - high], axis=0).astype(jnp.bfloat16)
    widen = spread(128, 128 * HPD, lambda i, j: j // HPD == i)
    r = lax.broadcasted_iota(jnp.int32, (2 * HPD, 128 * HPD), 0)
    cc = lax.broadcasted_iota(jnp.int32, (2 * HPD, 128 * HPD), 1)
    diagonal = r % HPD == cc % HPD
    total = jnp.zeros((2 * HPD, VDIM), jnp.float32)
    for g in range(4):
        wide = jnp.dot(both[:, g * 128 : (g + 1) * 128], widen, preferred_element_type=jnp.float32)
        wide = jnp.where(diagonal, wide, 0.0).astype(jnp.bfloat16)
        for j in range(4):
            slot = (4 * g + j - z + 4 + NZ) % NZ
            vals = w[slot // 4, slot % 4, :, :, :, NOPE:WIDTH].astype(jnp.float32).reshape(32 * HPD, VDIM)
            total += jnp.dot(
                wide[:, j * 256 : (j + 1) * 256], vals.astype(jnp.bfloat16), preferred_element_type=jnp.float32
            )
    attn[0] = (total[0:HPD] + total[HPD:]).astype(jnp.bfloat16)
    for cp in copies:
        cp.wait()


def per_device(kv_weight, queries, kv_cache, lengths):
    rows = kv_weight.shape[0]
    kvw = kv_weight.reshape(rows, NZ, HPD, WIDTH)
    kth = jnp.swapaxes(kv_cache, 1, 2)
    count = kth.shape[2]
    dma = pltpu.SemaphoreType.DMA
    bf16, f32 = jnp.bfloat16, jnp.float32
    vmem = pl.BlockSpec(memory_space=pltpu.VMEM)
    hbm = pl.BlockSpec(memory_space=pltpu.HBM)
    shape = (4, 4, NY, 4, HPD, WIDTH)
    w, lat = pl.pallas_call(
        gather_kernel,
        out_shape=(pltpu.VMEM(shape, bf16), pltpu.VMEM((HPD, KVL), f32)),
        in_specs=[hbm, hbm, hbm, hbm],
        out_specs=(vmem, vmem),
        scratch_shapes=[
            pltpu.VMEM((2, NZ, HPD, WIDTH), bf16),
            pltpu.VMEM((NZ, 2, HPD, NOPE), bf16),
            pltpu.VMEM((7, 2, HPD, NOPE), bf16),
            pltpu.VMEM((2, 2, HPD, WIDTH), bf16),
            pltpu.VMEM((KVL + ROPE, count), bf16),
            pltpu.VMEM((HPD, NOPE + ROPE), bf16),
            pltpu.SMEM((1,), jnp.int32),
            pltpu.VMEM((4, HPD, NOPE), bf16),
            pltpu.VMEM((4, HPD, 128), bf16),
            pltpu.VMEM((16, HPD, 128), bf16),
            pltpu.VMEM((HPD, KVL + 128), f32),
            pltpu.VMEM((3, HPD, KVL + 128), f32),
            dma((7,)), dma, dma, dma, dma, dma, dma((6,)), dma((4,)), dma((2,)), dma, dma,
            dma((2,)), dma((2,)), dma((2,)), dma((2, 4)), dma((2,)), dma((2,)), dma, dma, dma, dma, dma, dma,
        ],
        compiler_params=pltpu.CompilerParams(collective_id=0, has_side_effects=True),
        name="gather",
    )(kvw, queries, kth, lengths)
    w = pltpu.with_memory_space_constraint(w, pltpu.VMEM)
    lat = pltpu.with_memory_space_constraint(lat, pltpu.VMEM)
    out, attn = pl.pallas_call(
        project_kernel,
        out_shape=(jax.ShapeDtypeStruct((NZ, NY, 4, HPD, WIDTH), bf16), jax.ShapeDtypeStruct((1, HPD, VDIM), bf16)),
        in_specs=[vmem, vmem],
        out_specs=(hbm, vmem),
        scratch_shapes=[dma((NZ,))],
        name="project",
    )(w, lat)
    return out.reshape(KVL, HPD, WIDTH), attn


def solution(mesh):
    in_specs = (P(("dp", "mp"), None, None), P("rep", "dp", None), P("rep", "mp", None), P("rep"))
    out_specs = (P(None, "dp", None), P("rep", "dp", None))
    return jax.shard_map(per_device, mesh=mesh, in_specs=in_specs, out_specs=out_specs, check_vma=False)
```

time: 62.3 us -> 53.6 us (0.86)
  Pallas kernels: 60.8 us -> 52.1 us
    pallas_call x2, Pallas kernels: 60.8 us -> 52.1 us  [the longest x1 49.6 us: per_device(): pl.pallas_call(gather_kernel, out_shape=(pltpu.VMEM(shape, bf16), pltpu.V...]
where the time goes in v2:
time: 53.6 us; the launch traced here: 53.4 us
  Pallas kernels  52.1 us (97%)
  between operations  1.28 us (2%)
    pallas_call x1, Pallas kernels, per_device(): pl.pallas_call(gather_kernel, out_shape=(pltpu.VMEM(shape, bf16), pltpu.V...  49.6 us
    pallas_call x1, Pallas kernels, per_device(): pl.pallas_call(project_kernel, out_shape=(jax.ShapeDtypeStruct((NZ, NY, 4...  2.48 us

profile of v2, /device:TPU:1, one launch (start us, length us, event | category | flops | bytes accessed | tf_op | source)
XLA Modules:
  0.0 53.4 jit_solution(3290514384708158922)
XLA Ops:
  1.3 49.6 %gather.1 = (bf16[4,4,8,4,8,256]{5,4,3,2,1,0:T(8,128)(2,1)S(1)}, f32[8,512]{1,0:T(8,128)S(1)}) custom-call(bf16[8,16,8,256]{3,2,1,0:T(8,128)(2,1)} %bitcast.4, bf16[1,8,192]{2,1,0:T(8,128)(2,1)} %qh.1, bf16[1,576,1024]{2,1,0:T(8,128)(2,1)} %bitcast.3, s32[1]{0:T(128)S(6)} %copy.6.lenh), custom_call_target="tpu_custom_call" | custom-call | tf_op jit(solution)/shard_map/gather/pallas_call | solution.py:349
  50.9 2.5 %project.1 = (bf16[16,8,4,8,256]{4,3,2,1,0:T(8,128)(2,1)}, bf16[1,8,128]{2,1,0:T(8,128)(2,1)}) custom-call(bf16[4,4,8,4,8,256]{5,4,3,2,1,0:T(8,128)(2,1)S(1)} %get-tuple-element.6.w, f32[8,512]{1,0:T(8,128)S(1)} %get-tuple-element.7.lat), custom_call_target="tpu_custom_call" | custom-call | tf_op jit(solution)/shard_map/project/pallas_call | solution.py:375

commit v3 on v2

--- a/solution.py
+++ b/solution.py
@@ -30,8 +30,8 @@
 
 
 def gather_kernel(
-    kvw, qh, kth, lenh, w, lat,
-    share, zkeys, relay_k, relay_v, kt, qv, lens, qall, ab_send, ab_recv, mg_send, mg_recv,
+    kvw, qh, kth, lenh, w, wide,
+    perm, pick, widen, share, zkeys, relay_k, relay_v, kt, qv, lens, qall, ab_send, ab_recv, mg_send, mg_recv,
     loc, zs, zn, zr, zf, fs, vs, vr, vq, qs, qr, ys, yr, xs, xf, xb, xq, cs, cr, a_s, a_r, m_s, m_r,
 ):
     z = lax.axis_index("dp")
@@ -90,6 +90,13 @@
     own_q.start()
     own_k = local(share.at[:, z, :, key], zkeys.at[4], loc.at[5])
     own_k.start()
+
+    def place(i, j):
+        return j == ((((i >> 1) & 15) * 32 + (i >> 5) * 2 + (i & 1) + 32 * ((z + 12) % NZ)) & (KVL - 1))
+
+    perm[...] = spread(KVL, KVL, place)
+    pick[...] = spread(2 * NZ * HPD, 128, lambda i, j: j == 32 * (me % 4) + (i >> 3))
+    widen[...] = spread(128, 128 * HPD, lambda i, j: (j >> 3) == i)
     pl.semaphore_wait(barrier, len(REACH) + 15 + 2)
 
     def piece(d):
@@ -98,10 +105,6 @@
     def key_piece(d):
         return share.at[:, (z + d + 2 * NZ) % NZ, :, key]
 
-    for n, d in enumerate(FAR_D):
-        remote(key_piece(d), relay_k.at[n], zs, zr, zdev(4 if d > 0 else -4)).start()
-    for d in REACH:
-        remote(key_piece(d), zkeys.at[(4 - d) % NZ], zs, zn, zdev(d)).start()
     up = remote(piece(8 - x), relay_v.at[1], vs.at[3], vq.at[1], zdev(4))
     down = remote(piece(-4 - x), relay_v.at[0], vs.at[2], vq.at[0], zdev(-4))
     ahead = remote(piece(4 - x), w.at[0, x, y, pair], vs.at[0], vr.at[0], zdev(4 - x))
@@ -119,6 +122,11 @@
     def _():
         behind_own.start()
 
+    for n, d in enumerate(FAR_D):
+        remote(key_piece(d), relay_k.at[n], zs, zr, zdev(4 if d > 0 else -4)).start()
+    for d in REACH:
+        remote(key_piece(d), zkeys.at[(4 - d) % NZ], zs, zn, zdev(d)).start()
+
     for dl, dc in ((0, 1), (1, 0), (1, 1)):
         to = dev(z, 2 * m + (ylo + dl) % 2, (c + dc) % 2)
         remote(qv.at[:, pl.ds(0, NOPE)], qall.at[s], qs, qr, to).start()
@@ -128,60 +136,63 @@
     down_own = local(relay_v.at[0], w.at[2, x, y, pair], vr.at[2])
 
     def forward_far():
+        up.wait_recv()
+        up_rest.start()
+        down.wait_recv()
+
+        @pl.when(x > 0)
+        def _():
+            down_rest.start()
+
+        @pl.when(x == 0)
+        def _():
+            down_own.start()
+
+    def forward_keys():
         wait_all(zr, relay_k)
         for n, d in enumerate(FAR_D):
             rest = d - 4 if d > 0 else d + 4
             remote(relay_k.at[n], zkeys.at[(4 - d) % NZ], fs, zf, zdev(rest)).start()
-        up.wait_recv()
-        up_rest.start()
-        down.wait_recv()
-
-        @pl.when(x > 0)
-        def _():
-            down_rest.start()
-
-        @pl.when(x == 0)
-        def _():
-            down_own.start()
 
     def chunk(g, src):
         return w.at[pl.ds(2 * g, 2), x, src, pair]
 
     def to_y(g):
         for n in (4, 3, 5, 2, 6, 1, 7):
-            remote(chunk(g, y), chunk(g, y), ys.at[g], yr.at[g], dev(z, (y + n) % NY, c)).start()
+            remote(chunk(g, y), chunk(g, y), ys.at[g], yr.at[g, n], dev(z, (y + n) % NY, c)).start()
 
     def near_ready():
-        wait_all(zn, zkeys.at[pl.ds(0, 8)])
-        own_k.wait()
         ahead.wait_recv()
         behind.wait_recv()
         to_y(NEAR)
-
-    def far_keys():
-        wait_all(zf, relay_k)
 
     def far_ready():
         up_rest.wait_recv()
         down_rest.wait_recv()
         to_y(FAR)
 
+    def all_keys():
+        wait_all(zf, relay_k)
+        wait_all(zn, zkeys.at[pl.ds(0, 8)])
+        own_k.wait()
+
     def part(g, n, b):
-        return w.at[2 * g + n // 2, b, pl.ds(4 * (n % 2), 4), pair]
-
-    def to_x(g):
-        wait_all(yr.at[g], w.at[0, 0, pl.ds(0, 7)])
-        for n in range(4):
+        return w.at[pl.ds(2 * g, 2), b, (y - n + NY) % NY, pair]
+
+    def send_x(g, *ns):
+        for n in ns:
+            if n:
+                wait_all(yr.at[g, n], chunk(g, y))
             ref = part(g, n, x)
             remote(ref, ref, xs.at[g], xf.at[g, n], xdev(sg)).start()
             remote(ref, ref, xs.at[g], xb.at[g], xdev(-sg)).start()
-        to_core(g, x)
-
-    def relay_x(g, n):
-        ref = part(g, n, (x - sg + NX) % NX)
-        cp = remote(ref, ref, xs.at[g], xf.at[g, n], xdev(sg))
-        cp.wait_recv()
-        remote(ref, ref, xs.at[g], xq.at[g], xdev(sg)).start()
+
+    def relay_x(g, *ns):
+        for n in ns:
+            ref = part(g, n, (x - sg + NX) % NX)
+            cp = remote(ref, ref, xs.at[g], xf.at[g, n], xdev(sg))
+            cp.wait_recv()
+            remote(ref, ref, xs.at[g], xq.at[g], xdev(sg)).start()
 
     def to_core(g, b):
         ref = w.at[pl.ds(2 * g, 2), b, :, pair]
@@ -209,10 +220,8 @@
         )
         r = lax.broadcasted_iota(jnp.int32, cross.shape, 0)
         cc = lax.broadcasted_iota(jnp.int32, cross.shape, 1)
-        own = jnp.where(r % HPD == cc % HPD, cross, 0.0).astype(jnp.bfloat16)
-        base = 32 * (me % 4)
-        pick = spread(2 * NZ * HPD, 128, lambda i, j: j == base + i // HPD)
-        packed = jnp.dot(own, pick, preferred_element_type=jnp.float32)
+        own = jnp.where((r & (HPD - 1)) == (cc & (HPD - 1)), cross, 0.0).astype(jnp.bfloat16)
+        packed = jnp.dot(own, pick[...], preferred_element_type=jnp.float32)
         ab_send[...] = packed.reshape(4, HPD, 128).astype(jnp.bfloat16)
         own_ab.start()
         for n in (8, 9, 7, 10, 6, 11, 5, 12, 4, 13, 3, 14, 2, 15, 1):
@@ -222,18 +231,13 @@
     own_ab = local(ab_send.at[s], ab_recv.at[me], loc.at[6])
 
     def attend():
-        def place(i, j):
-            src, slot, row = i // 32, (i % 32) // 2, i % 2
-            return j == ((slot + z + 12) % NZ) * 32 + src * 2 + row
-
-        perm = spread(KVL, KVL, place)
         fetch_kt.wait()
         fetch_l.wait()
         own_ab.wait()
         wait_all(a_r, ab_recv.at[pl.ds(0, 15)])
         tiles = [sum(ab_recv[4 * g + j].astype(jnp.float32) for j in range(4)) for g in range(4)]
         got = jnp.concatenate(tiles, axis=1).astype(jnp.bfloat16)
-        absorbed = jnp.dot(got, perm, preferred_element_type=jnp.float32).astype(jnp.bfloat16)
+        absorbed = jnp.dot(got, perm[...], preferred_element_type=jnp.float32).astype(jnp.bfloat16)
         scores = jnp.dot(absorbed, kt[0:KVL, :], preferred_element_type=jnp.float32)
         scores += jnp.dot(qv[:, NOPE : NOPE + ROPE], kt[KVL : KVL + ROPE, :], preferred_element_type=jnp.float32)
         scores = scores * ((NOPE + ROPE) ** (-0.5))
@@ -264,23 +268,38 @@
         factors = [jnp.exp(t - top) for t in tops]
         total = sum(f * t for f, t in zip(factors, totals))
         value = sum(f * p[:, 0:KVL] for f, p in zip(factors, parts))
-        lat[...] = value / total
+        value = value / total
+        high = value.astype(jnp.bfloat16).astype(jnp.float32)
+        both = jnp.concatenate([high, value - high], axis=0).astype(jnp.bfloat16)
+        r = lax.broadcasted_iota(jnp.int32, (2 * HPD, 128 * HPD), 0)
+        cc = lax.broadcasted_iota(jnp.int32, (2 * HPD, 128 * HPD), 1)
+        diagonal = (r & (HPD - 1)) == (cc & (HPD - 1))
+        for g in range(4):
+            wider = jnp.dot(both[:, g * 128 : (g + 1) * 128], widen[...], preferred_element_type=jnp.float32)
+            wide[g] = jnp.where(diagonal, wider, 0.0).astype(jnp.bfloat16)
 
     forward_far()
     near_ready()
-    far_keys()
+    send_x(NEAR, 0)
+    forward_keys()
+    send_x(NEAR, 1, 7, 2, 6)
     far_ready()
+    send_x(FAR, 0)
+    all_keys()
     absorb()
-    to_x(NEAR)
-    for n in range(4):
-        relay_x(NEAR, n)
+    send_x(NEAR, 3, 5, 4)
+    relay_x(NEAR, 0, 1, 7, 2, 6)
+    to_core(NEAR, x)
+    send_x(FAR, 1, 7, 2, 6)
+    relay_x(NEAR, 3, 5, 4)
     attend()
-    to_x(FAR)
+    send_x(FAR, 3, 5, 4)
+    relay_x(FAR, 0, 1, 7, 2, 6)
+    to_core(FAR, x)
     behind_x(NEAR)
     other_x(NEAR)
     across_x(NEAR)
-    for n in range(4):
-        relay_x(FAR, n)
+    relay_x(FAR, 3, 5, 4)
     behind_x(FAR)
     other_x(FAR)
     merge()
@@ -306,7 +325,7 @@
     wait_all(m_s, mg_recv)
 
 
-def project_kernel(w, lat, out, attn, sems):
+def project_kernel(w, wide, out, attn, sems):
     z = lax.axis_index("dp")
     copies = []
     for i in range(NZ):
@@ -314,23 +333,11 @@
         cp = pltpu.make_async_copy(w.at[slot // 4, slot % 4], out.at[i], sems.at[i])
         cp.start()
         copies.append(cp)
-    value = lat[...]
-    high = value.astype(jnp.bfloat16).astype(jnp.float32)
-    both = jnp.concatenate([high, value - high], axis=0).astype(jnp.bfloat16)
-    widen = spread(128, 128 * HPD, lambda i, j: j // HPD == i)
-    r = lax.broadcasted_iota(jnp.int32, (2 * HPD, 128 * HPD), 0)
-    cc = lax.broadcasted_iota(jnp.int32, (2 * HPD, 128 * HPD), 1)
-    diagonal = r % HPD == cc % HPD
     total = jnp.zeros((2 * HPD, VDIM), jnp.float32)
-    for g in range(4):
-        wide = jnp.dot(both[:, g * 128 : (g + 1) * 128], widen, preferred_element_type=jnp.float32)
-        wide = jnp.where(diagonal, wide, 0.0).astype(jnp.bfloat16)
-        for j in range(4):
-            slot = (4 * g + j - z + 4 + NZ) % NZ
-            vals = w[slot // 4, slot % 4, :, :, :, NOPE:WIDTH].astype(jnp.float32).reshape(32 * HPD, VDIM)
-            total += jnp.dot(
-                wide[:, j * 256 : (j + 1) * 256], vals.astype(jnp.bfloat16), preferred_element_type=jnp.float32
-            )
+    for i in range(NZ):
+        slot = (i - z + 4 + NZ) % NZ
+        vals = w[slot // 4, slot % 4, :, :, :, NOPE:WIDTH].reshape(32 * HPD, VDIM)
+        total += jnp.dot(wide[i // 4, :, (i % 4) * 256 : (i % 4 + 1) * 256], vals, preferred_element_type=jnp.float32)
     attn[0] = (total[0:HPD] + total[HPD:]).astype(jnp.bfloat16)
     for cp in copies:
         cp.wait()
@@ -346,12 +353,15 @@
     vmem = pl.BlockSpec(memory_space=pltpu.VMEM)
     hbm = pl.BlockSpec(memory_space=pltpu.HBM)
     shape = (4, 4, NY, 4, HPD, WIDTH)
-    w, lat = pl.pallas_call(
+    w, wide = pl.pallas_call(
         gather_kernel,
-        out_shape=(pltpu.VMEM(shape, bf16), pltpu.VMEM((HPD, KVL), f32)),
+        out_shape=(pltpu.VMEM(shape, bf16), pltpu.VMEM((4, 2 * HPD, 128 * HPD), bf16)),
         in_specs=[hbm, hbm, hbm, hbm],
         out_specs=(vmem, vmem),
         scratch_shapes=[
+            pltpu.VMEM((KVL, KVL), bf16),
+            pltpu.VMEM((2 * NZ * HPD, 128), bf16),
+            pltpu.VMEM((128, 128 * HPD), bf16),
             pltpu.VMEM((2, NZ, HPD, WIDTH), bf16),
             pltpu.VMEM((NZ, 2, HPD, NOPE), bf16),
             pltpu.VMEM((7, 2, HPD, NOPE), bf16),
@@ -365,13 +375,13 @@
             pltpu.VMEM((HPD, KVL + 128), f32),
             pltpu.VMEM((3, HPD, KVL + 128), f32),
             dma((7,)), dma, dma, dma, dma, dma, dma((6,)), dma((4,)), dma((2,)), dma, dma,
-            dma((2,)), dma((2,)), dma((2,)), dma((2, 4)), dma((2,)), dma((2,)), dma, dma, dma, dma, dma, dma,
+            dma((2,)), dma((2, 8)), dma((2,)), dma((2, 8)), dma((2,)), dma((2,)), dma, dma, dma, dma, dma, dma,
         ],
         compiler_params=pltpu.CompilerParams(collective_id=0, has_side_effects=True),
         name="gather",
     )(kvw, queries, kth, lengths)
     w = pltpu.with_memory_space_constraint(w, pltpu.VMEM)
-    lat = pltpu.with_memory_space_constraint(lat, pltpu.VMEM)
+    wide = pltpu.with_memory_space_constraint(wide, pltpu.VMEM)
     out, attn = pl.pallas_call(
         project_kernel,
         out_shape=(jax.ShapeDtypeStruct((NZ, NY, 4, HPD, WIDTH), bf16), jax.ShapeDtypeStruct((1, HPD, VDIM), bf16)),
@@ -379,7 +389,7 @@
         out_specs=(hbm, vmem),
         scratch_shapes=[dma((NZ,))],
         name="project",
-    )(w, lat)
+    )(w, wide)
     return out.reshape(KVL, HPD, WIDTH), attn
 
 

time: 53.6 us -> 51.4 us (0.959)
  Pallas kernels: 52.1 us -> 50 us
    pallas_call x1, Pallas kernels: 49.6 us -> 47.8 us  [per_device(): pl.pallas_call(gather_kernel, out_shape=(pltpu.VMEM(shape, bf16), pltpu.V...]
where the time goes in v3:
time: 51.4 us; the launch traced here: 51.2 us
  Pallas kernels  50 us (97%)
  between operations  1.28 us (2%)
    pallas_call x1, Pallas kernels, per_device(): pl.pallas_call(gather_kernel, out_shape=(pltpu.VMEM(shape, bf16), pltpu.V...  47.8 us
    pallas_call x1, Pallas kernels, per_device(): pl.pallas_call(project_kernel, out_shape=(jax.ShapeDtypeStruct((NZ, NY, 4...  2.2 us

profile of v3, /device:TPU:1, one launch (start us, length us, event | category | flops | bytes accessed | tf_op | source)
XLA Modules:
  0.0 51.2 jit_solution(1767561569220731632)
XLA Ops:
  1.3 47.8 %gather.1 = (bf16[4,4,8,4,8,256]{5,4,3,2,1,0:T(8,128)(2,1)S(1)}, bf16[4,16,1024]{2,1,0:T(8,128)(2,1)S(1)}) custom-call(bf16[8,16,8,256]{3,2,1,0:T(8,128)(2,1)} %bitcast.4, bf16[1,8,192]{2,1,0:T(8,128)(2,1)} %qh.1, bf16[1,576,1024]{2,1,0:T(8,128)(2,1)} %bitcast.3, s32[1]{0:T(128)S(6)} %copy.6.lenh), custom_call_target="tpu_custom_call" | custom-call | tf_op jit(solution)/shard_map/gather/pallas_call | solution.py:356
  49.0 2.2 %project.1 = (bf16[16,8,4,8,256]{4,3,2,1,0:T(8,128)(2,1)}, bf16[1,8,128]{2,1,0:T(8,128)(2,1)}) custom-call(bf16[4,4,8,4,8,256]{5,4,3,2,1,0:T(8,128)(2,1)S(1)} %get-tuple-element.6.w, bf16[4,16,1024]{2,1,0:T(8,128)(2,1)S(1)} %get-tuple-element.7.wide), custom_call_target="tpu_custom_call" | custom-call | tf_op jit(solution)/shard_map/project/pallas_call | solution.py:385

commit v4 on v3

--- a/solution.py
+++ b/solution.py
@@ -288,20 +288,17 @@
     all_keys()
     absorb()
     send_x(NEAR, 3, 5, 4)
-    relay_x(NEAR, 0, 1, 7, 2, 6)
     to_core(NEAR, x)
-    send_x(FAR, 1, 7, 2, 6)
-    relay_x(NEAR, 3, 5, 4)
+    send_x(FAR, 1, 7, 2, 6, 3, 5, 4)
+    to_core(FAR, x)
     attend()
-    send_x(FAR, 3, 5, 4)
-    relay_x(FAR, 0, 1, 7, 2, 6)
-    to_core(FAR, x)
+    relay_x(NEAR, 0, 1, 7, 2, 6, 3, 5, 4)
     behind_x(NEAR)
+    relay_x(FAR, 0, 1, 7, 2, 6, 3, 5, 4)
+    behind_x(FAR)
     other_x(NEAR)
+    other_x(FAR)
     across_x(NEAR)
-    relay_x(FAR, 3, 5, 4)
-    behind_x(FAR)
-    other_x(FAR)
     merge()
     across_x(FAR)
     wait_all(cr, w.at[pl.ds(0, 2)])

time: 51.4 us -> 50.5 us (0.982)
  Pallas kernels: 50 us -> 49.1 us
    pallas_call x1, Pallas kernels: 47.8 us -> 46.9 us  [per_device(): pl.pallas_call(gather_kernel, out_shape=(pltpu.VMEM(shape, bf16), pltpu.V...]
where the time goes in v4:
time: 50.5 us; the launch traced here: 50.4 us
  Pallas kernels  49.1 us (97%)
  between operations  1.28 us (3%)
    pallas_call x1, Pallas kernels, per_device(): pl.pallas_call(gather_kernel, out_shape=(pltpu.VMEM(shape, bf16), pltpu.V...  46.9 us
    pallas_call x1, Pallas kernels, per_device(): pl.pallas_call(project_kernel, out_shape=(jax.ShapeDtypeStruct((NZ, NY, 4...  2.2 us

profile of v4, /device:TPU:1, one launch (start us, length us, event | category | flops | bytes accessed | tf_op | source)
XLA Modules:
  0.0 50.4 jit_solution(3747107076080046516)
XLA Ops:
  1.3 46.9 %gather.1 = (bf16[4,4,8,4,8,256]{5,4,3,2,1,0:T(8,128)(2,1)S(1)}, bf16[4,16,1024]{2,1,0:T(8,128)(2,1)S(1)}) custom-call(bf16[8,16,8,256]{3,2,1,0:T(8,128)(2,1)} %bitcast.4, bf16[1,8,192]{2,1,0:T(8,128)(2,1)} %qh.1, bf16[1,576,1024]{2,1,0:T(8,128)(2,1)} %bitcast.3, s32[1]{0:T(128)S(6)} %copy.6.lenh), custom_call_target="tpu_custom_call" | custom-call | tf_op jit(solution)/shard_map/gather/pallas_call | solution.py:353
  48.2 2.2 %project.1 = (bf16[16,8,4,8,256]{4,3,2,1,0:T(8,128)(2,1)}, bf16[1,8,128]{2,1,0:T(8,128)(2,1)}) custom-call(bf16[4,4,8,4,8,256]{5,4,3,2,1,0:T(8,128)(2,1)S(1)} %get-tuple-element.6.w, bf16[4,16,1024]{2,1,0:T(8,128)(2,1)S(1)} %get-tuple-element.7.wide), custom_call_target="tpu_custom_call" | custom-call | tf_op jit(solution)/shard_map/project/pallas_call | solution.py:382
